TPU v7x, 32 devices: a whole 2x2x4 slice. The times are simulated.
32 devices in a mesh: row: 4 (over y, x), col: 8 (over z, core).
Axes of the slice: x: 2, y: 2, z: 4, core: 2. Of those that a mesh axis runs over, the one named last changes fastest.
Arguments:
- integrals: bfloat16 [2880, 23040], P('row', 'col'), may hold values from -0.0390625 to 0.0390625
- amplitudes: bfloat16 [23040, 256], P('col', 'row'), may hold values from -6 to 6
Outputs:
- ladder: bfloat16 [256, 2880], P('col', 'row')
All inputs are finite; a program needn't handle non-finite values.
Results may differ from a plain program's by a relative error of at most 0.001.
Values may be sent and summed in bfloat16 or wider, within the bound.
A program may use at most 64 MiB of HBM per device.

v0:
```python
import jax
import jax.numpy as jnp
from jax import lax
from jax.sharding import PartitionSpec as P


def per_device(integrals, amplitudes):
    columns = lax.axis_size("col")
    gathered = lax.all_gather(amplitudes, "row", axis=1, tiled=True)
    local_rows = integrals.shape[0]
    row_count = (local_rows + columns - 1) // columns
    padded_rows = row_count * columns
    padded = jnp.pad(integrals, ((0, padded_rows - local_rows), (0, 0)))
    totals = lax.psum_scatter(
        jnp.dot(padded, gathered, preferred_element_type=jnp.float32),
        "col",
        scatter_dimension=0,
        tiled=True,
    ).astype(jnp.bfloat16)
    regrouped = lax.all_to_all(totals, "col", split_axis=1, concat_axis=0, tiled=True)
    return regrouped[:local_rows].T


def solution(mesh):
    in_specs = (P("row", "col"), P("col", "row"))
    out_specs = P("col", "row")
    return jax.shard_map(
        per_device, mesh=mesh, in_specs=in_specs, out_specs=out_specs, check_vma=False
    )
```

profile of v0, /device:TPU:0, one launch (start us, length us, event | category | flops | bytes accessed | tf_op | source)
XLA Modules:
  0.0 86.1 jit_solution(9630065998873702536)
XLA Ops:
  6.5 0.0 all-gather.2.cloned.1.call-start
  6.5 0.7 all-gather.2.cloned.1.call-update
  7.3 0.0 copy-start
  7.3 35.0 %all-gather.2.cloned.1.call-done = bf16[2880,256]{0,1:T(8,128)(2,1)} async-done(((bf16[2880,64]{0,1:T(8,128)(2,1)}), bf16[2880,256]{0,1:T(8,128)(2,1)}) %all-gather.2.cloned.1.call-update) | async-done | bytes 1474576 | tf_op jit(solution)/shard_map/all_gather | solution.py:9
  42.2 4.0 %fusion.1 = f32[720,256]{1,0:T(8,128)S(1)} fusion(bf16[720,2880]{1,0:T(8,128)(2,1)} %param.2, bf16[2880,256]{0,1:T(8,128)(2,1)} %all-gather.2.cloned.1.call-done), kind=kOutput, calls=%fused_computation.1 | convolution fusion | flops 1061683200 | bytes 6359040 | tf_op jit(solution)/shard_map/dot_general | solution.py:15
  46.2 20.7 %fusion = f32[96,256]{1,0:T(8,128)S(1)} fusion(f32[720,256]{1,0:T(8,128)S(1)} %fusion.1), kind=kCustom, calls=%all-reduce-scatter | all-reduce-scatter fusion | flops 196609 | bytes 836096
  67.0 1.3 %collective-permute-start = (bf16[42,256]{1,0:T(8,128)(2,1)S(1)}, bf16[42,256]{1,0:T(8,128)(2,1)S(1)}, u32[]{:S(2)}, u32[]{:S(2)}) collective-permute-start(bf16[42,256]{1,0:T(8,128)(2,1)S(1)} %slice), channel_id=1, source_target_pairs={{0,1},{1,2},{2,3},{3,4},{4,5},{5,6},{6,7},{8,9},{9,10},{10,11},{11... | collective-permute-start | bytes 64520
  68.3 0.0 copy-done
  68.3 0.6 dynamic-slice.4
  69.5 0.0 collective-permute-done
  69.5 0.3 concatenate
  69.8 0.1 copy.7
  70.0 8.5 %all_to_all.19 = bf16[90,8,32]{0,2,1:T(8,128)(2,1)S(1)} all-to-all(bf16[90,8,32]{0,2,1:T(8,128)(2,1)S(1)} %bitcast.10), channel_id=1, replica_groups=mesh['row'=4,'col'=8] {'col'}, dimensions={1} | all-to-all | bytes 92160 | tf_op jit(solution)/shard_map/all_to_all | solution.py:20
  78.5 0.7 all_to_all.17
  (3 shorter events, 0.1 us)
Async XLA Ops:
  6.5 35.7 %all-gather.2.cloned.1.call-start = ((), (), s32[]{:S(2)}) async-start(), calls=%async_computation.1 | async-start | bytes 1884160 | tf_op jit(solution)/shard_map/all_gather | solution.py:9
  7.3 61.0 %copy-start = (u32[32]{0:T(128)S(1)}, u32[32]{0:T(128)}, u32[]{:S(2)}) copy-start(u32[32]{0:T(128)} %constant.3) | copy-start | bytes 388
  67.0 2.6 %collective-permute-start = (bf16[42,256]{1,0:T(8,128)(2,1)S(1)}, bf16[42,256]{1,0:T(8,128)(2,1)S(1)}, u32[]{:S(2)}, u32[]{:S(2)}) collective-permute-start(bf16[42,256]{1,0:T(8,128)(2,1)S(1)} %slice), channel_id=1, source_target_pairs={{0,1},{1,2},{2,3},{3,4},{4,5},{5,6},{6,7},{8,9},{9,10},{10,11},{11... | collective-permute-start | bytes 64520
Sparse Core Ops, SparseCore 0:
  9.2 33.0 all-gather.1
where the time goes:
time: 86.3 us; the launch traced here: 86.1 us
  waiting for transfers between devices  35.7 us (41%)
  blocking collectives  29.2 us (34%)
  between operations  14.1 us (16%)
  matrix products  4 us (5%)
  local copies, waits for them, and re-layouts  1.76 us (2%)
  starting transfers between devices  1.29 us (1%)
    all_gather x1, waiting for transfers between devices, per_device(): gathered = lax.all_gather(amplitudes, 'row', axis=1, tiled=True)  35 us
    unnamed x1, blocking collectives  20.7 us
    all_to_all x1, blocking collectives, per_device(): lax.all_to_all(totals, 'col', split_axis=1, concat_axis=0, tiled=True)  8.52 us
    dot_general x1, matrix products, per_device(): jnp.dot(padded, gathered, preferred_element_type=jnp.float32)  4 us
  transfers between devices with their start and end apart: 2, of which 1 were waited for; matrix products, arithmetic and copies ran while one was open for 1% of the time, Pallas kernels for 0%

commit v1 on v0

--- a/solution.py
+++ b/solution.py
@@ -2,6 +2,28 @@
 import jax.numpy as jnp
 from jax import lax
 from jax.sharding import PartitionSpec as P
+
+
+def split_up(x, dim, size):
+    before, after = (x.shape[:dim], x.shape[dim + 1 :])
+    return jnp.moveaxis(x.reshape(*before, size, -1, *after), dim, 0)
+
+
+def in_order(pieces, dim):
+    pieces = jnp.moveaxis(pieces, 0, dim)
+    shape = pieces.shape
+    return pieces.reshape(*shape[:dim], shape[dim] * shape[dim + 1], *shape[dim + 2 :])
+
+
+def swapped_with_each(value, axis, split_dim, concat_dim):
+    count, place = (lax.axis_size(axis), lax.axis_index(axis))
+    blocks = split_up(value, split_dim, count)
+    outs = [blocks[place]]
+    for step in range(1, count):
+        sent = blocks[place ^ step]
+        outs.append(lax.ppermute(sent, axis, [(i, i ^ step) for i in range(count)]))
+    blocks = jnp.stack(outs)[place ^ jnp.arange(count)]
+    return in_order(blocks, concat_dim)
 
 
 def per_device(integrals, amplitudes):
@@ -17,7 +39,7 @@
         scatter_dimension=0,
         tiled=True,
     ).astype(jnp.bfloat16)
-    regrouped = lax.all_to_all(totals, "col", split_axis=1, concat_axis=0, tiled=True)
+    regrouped = swapped_with_each(totals, "col", 1, 0)
     return regrouped[:local_rows].T
 
 

time: 86.3 us -> 89.3 us (1.035)
  blocking collectives: 29.2 us -> 20.7 us
  starting transfers between devices: 1.29 us -> 9.39 us
  waiting for transfers between devices: 35.7 us -> 38.3 us
    all_to_all x1 -> x0, blocking collectives: 8.52 us -> none  [per_device(): lax.all_to_all(totals, 'col', split_axis=1, concat_axis=0, tiled=True)]
    ppermute x0 -> x7, starting transfers between devices: none -> 8.09 us  [swapped_with_each(): outs.append(lax.ppermute(sent, axis, [(i, i ^ step) for i in range(count)]))]
    ppermute x0 -> x7, waiting for transfers between devices: none -> 2.7 us  [swapped_with_each(): outs.append(lax.ppermute(sent, axis, [(i, i ^ step) for i in range(count)]))]
  transfers between devices with their start and end apart: 2 -> 9, of which waited for: 1 -> 3; matrix products, arithmetic and copies ran while one was open for 1% -> 1% of each run, Pallas kernels for 0% -> 0%
where the time goes in v1:
time: 89.3 us; the launch traced here: 89.2 us
  waiting for transfers between devices  38.3 us (43%)
  blocking collectives  20.7 us (23%)
  between operations  14.3 us (16%)
  starting transfers between devices  9.39 us (11%)
  matrix products  4 us (4%)
  local copies, waits for them, and re-layouts  2.41 us (3%)
    all_gather x1, waiting for transfers between devices, per_device(): gathered = lax.all_gather(amplitudes, 'row', axis=1, tiled=True)  34.9 us
    unnamed x1, blocking collectives  20.7 us
    ppermute x7, starting transfers between devices, swapped_with_each(): outs.append(lax.ppermute(sent, axis, [(i, i ^ step) for i in range(count)]))  8.09 us
    dot_general x1, matrix products, per_device(): jnp.dot(padded, gathered, preferred_element_type=jnp.float32)  4 us
    ppermute x7, waiting for transfers between devices, swapped_with_each(): outs.append(lax.ppermute(sent, axis, [(i, i ^ step) for i in range(count)]))  2.7 us
  transfers between devices with their start and end apart: 9, of which 3 were waited for; matrix products, arithmetic and copies ran while one was open for 1% of the time, Pallas kernels for 0%

profile of v1, /device:TPU:0, one launch (start us, length us, event | category | flops | bytes accessed | tf_op | source)
XLA Modules:
  0.0 89.2 jit_solution(11442755185314969760)
XLA Ops:
  6.5 0.0 all-gather.2.cloned.1.call-start
  6.5 0.7 all-gather.2.cloned.1.call-update
  7.3 0.0 copy-start
  7.3 34.9 %all-gather.2.cloned.1.call-done = bf16[2880,256]{0,1:T(8,128)(2,1)} async-done(((bf16[2880,64]{0,1:T(8,128)(2,1)}), bf16[2880,256]{0,1:T(8,128)(2,1)}) %all-gather.2.cloned.1.call-update) | async-done | bytes 1474576 | tf_op jit(solution)/shard_map/all_gather | solution.py:31
  42.2 4.0 %fusion.2 = f32[720,256]{1,0:T(8,128)S(1)} fusion(bf16[720,2880]{1,0:T(8,128)(2,1)} %param.2, bf16[2880,256]{0,1:T(8,128)(2,1)} %all-gather.2.cloned.1.call-done), kind=kOutput, calls=%fused_computation.20 | convolution fusion | flops 1061683200 | bytes 6359040 | tf_op jit(solution)/shard_map/dot_general | solution.py:37
  46.2 20.7 %fusion = f32[96,256]{1,0:T(8,128)S(1)} fusion(f32[720,256]{1,0:T(8,128)S(1)} %fusion.2), kind=kCustom, calls=%all-reduce-scatter | all-reduce-scatter fusion | flops 196609 | bytes 836096
  67.0 1.3 %collective-permute-start.7 = (bf16[42,256]{1,0:T(8,128)(2,1)S(1)}, bf16[42,256]{1,0:T(8,128)(2,1)S(1)}, u32[]{:S(2)}, u32[]{:S(2)}) collective-permute-start(bf16[42,256]{1,0:T(8,128)(2,1)S(1)} %slice.2), channel_id=1, source_target_pairs={{0,1},{1,2},{2,3},{3,4},{4,5},{5,6},{6,7},{8,9},{9,10},{10,11},{11... | collective-permute-start | bytes 64520
  68.3 0.0 copy-done
  68.3 0.6 dynamic-slice.36
  69.6 0.0 collective-permute-done.7
  69.6 0.3 concatenate
  69.9 0.1 copy.6
  70.1 0.1 collective-permute-start
  70.2 0.3 collective-permute-start.1
  70.4 1.6 %collective-permute-start.2 = (bf16[90,32]{0,1:T(8,128)(2,1)S(1)}, bf16[90,32]{0,1:T(8,128)(2,1)S(1)}, u32[]{:S(2)}, u32[]{:S(2)}) collective-permute-start(bf16[90,32]{0,1:T(8,128)(2,1)S(1)} %get-tuple-element.9), channel_id=1, source_target_pairs={{0,3},{1,2},{2,1},{3,0},{4,7},{5,6},{6,5},{7,4},{8,11},{9,10},{10,... | collective-permute-start | bytes 17288 | tf_op jit(solution)/shard_map/ppermute | solution.py:24
  72.0 0.6 collective-permute-start.3
  72.6 2.0 %collective-permute-start.4 = (bf16[90,32]{0,1:T(8,128)(2,1)S(1)}, bf16[90,32]{0,1:T(8,128)(2,1)S(1)}, u32[]{:S(2)}, u32[]{:S(2)}) collective-permute-start(bf16[90,32]{0,1:T(8,128)(2,1)S(1)} %get-tuple-element.7), channel_id=1, source_target_pairs={{0,5},{1,4},{2,7},{3,6},{4,1},{5,0},{6,3},{7,2},{8,13},{9,12},{10,... | collective-permute-start | bytes 17288 | tf_op jit(solution)/shard_map/ppermute | solution.py:24
  74.6 0.0 collective-permute-done
  74.6 1.4 %collective-permute-start.5 = (bf16[90,32]{0,1:T(8,128)(2,1)S(1)}, bf16[90,32]{0,1:T(8,128)(2,1)S(1)}, u32[]{:S(2)}, u32[]{:S(2)}) collective-permute-start(bf16[90,32]{0,1:T(8,128)(2,1)S(1)} %get-tuple-element.6), channel_id=1, source_target_pairs={{0,6},{1,7},{2,4},{3,5},{4,2},{5,3},{6,0},{7,1},{8,14},{9,15},{10,... | collective-permute-start | bytes 17288 | tf_op jit(solution)/shard_map/ppermute | solution.py:24
  76.1 0.0 collective-permute-done.1
  76.1 2.1 %collective-permute-start.6 = (bf16[90,32]{0,1:T(8,128)(2,1)S(1)}, bf16[90,32]{0,1:T(8,128)(2,1)S(1)}, u32[]{:S(2)}, u32[]{:S(2)}) collective-permute-start(bf16[90,32]{0,1:T(8,128)(2,1)S(1)} %get-tuple-element.5), channel_id=1, source_target_pairs={{0,7},{1,6},{2,5},{3,4},{4,3},{5,2},{6,1},{7,0},{8,15},{9,14},{10,... | collective-permute-start | bytes 17288 | tf_op jit(solution)/shard_map/ppermute | solution.py:24
  78.2 0.0 collective-permute-done.2
  78.2 0.0 collective-permute-done.3
  78.2 0.0 collective-permute-done.4
  78.3 1.8 %collective-permute-done.5 = bf16[90,32]{0,1:T(8,128)(2,1)S(1)} collective-permute-done((bf16[90,32]{0,1:T(8,128)(2,1)S(1)}, bf16[90,32]{0,1:T(8,128)(2,1)S(1)}, u32[]{:S(2)}, u32[]{:S(2)}) %collective-permute-start.5) | collective-permute-done | bytes 5792 | tf_op jit(solution)/shard_map/ppermute | solution.py:24
  80.1 0.9 collective-permute-done.6
  81.0 0.6 gather_fusion
  81.6 0.7 reshape.38
  (14 shorter events, 0.2 us)
Async XLA Ops:
  6.5 35.7 %all-gather.2.cloned.1.call-start = ((), (), s32[]{:S(2)}) async-start(), calls=%async_computation | async-start | bytes 1884160 | tf_op jit(solution)/shard_map/all_gather | solution.py:31
  7.3 61.1 %copy-start = (u32[32]{0:T(128)S(1)}, u32[32]{0:T(128)}, u32[]{:S(2)}) copy-start(u32[32]{0:T(128)} %constant.26) | copy-start | bytes 388
  67.0 2.6 %collective-permute-start.7 = (bf16[42,256]{1,0:T(8,128)(2,1)S(1)}, bf16[42,256]{1,0:T(8,128)(2,1)S(1)}, u32[]{:S(2)}, u32[]{:S(2)}) collective-permute-start(bf16[42,256]{1,0:T(8,128)(2,1)S(1)} %slice.2), channel_id=1, source_target_pairs={{0,1},{1,2},{2,3},{3,4},{4,5},{5,6},{6,7},{8,9},{9,10},{10,11},{11... | collective-permute-start | bytes 64520
  70.1 4.6 %collective-permute-start = (bf16[90,32]{0,1:T(8,128)(2,1)S(1)}, bf16[90,32]{0,1:T(8,128)(2,1)S(1)}, u32[]{:S(2)}, u32[]{:S(2)}) collective-permute-start(bf16[90,32]{0,1:T(8,128)(2,1)S(1)} %get-tuple-element.11), channel_id=1, source_target_pairs={{0,1},{1,0},{2,3},{3,2},{4,5},{5,4},{6,7},{7,6},{8,9},{9,8},{10,11... | collective-permute-start | bytes 17288 | tf_op jit(solution)/shard_map/ppermute | solution.py:24
  70.2 5.9 %collective-permute-start.1 = (bf16[90,32]{0,1:T(8,128)(2,1)S(1)}, bf16[90,32]{0,1:T(8,128)(2,1)S(1)}, u32[]{:S(2)}, u32[]{:S(2)}) collective-permute-start(bf16[90,32]{0,1:T(8,128)(2,1)S(1)} %get-tuple-element.10), channel_id=1, source_target_pairs={{0,2},{1,3},{2,0},{3,1},{4,6},{5,7},{6,4},{7,5},{8,10},{9,11},{10,... | collective-permute-start | bytes 17288 | tf_op jit(solution)/shard_map/ppermute | solution.py:24
  70.4 7.8 %collective-permute-start.2 = (bf16[90,32]{0,1:T(8,128)(2,1)S(1)}, bf16[90,32]{0,1:T(8,128)(2,1)S(1)}, u32[]{:S(2)}, u32[]{:S(2)}) collective-permute-start(bf16[90,32]{0,1:T(8,128)(2,1)S(1)} %get-tuple-element.9), channel_id=1, source_target_pairs={{0,3},{1,2},{2,1},{3,0},{4,7},{5,6},{6,5},{7,4},{8,11},{9,10},{10,... | collective-permute-start | bytes 17288 | tf_op jit(solution)/shard_map/ppermute | solution.py:24
  72.0 6.2 %collective-permute-start.3 = (bf16[90,32]{0,1:T(8,128)(2,1)S(1)}, bf16[90,32]{0,1:T(8,128)(2,1)S(1)}, u32[]{:S(2)}, u32[]{:S(2)}) collective-permute-start(bf16[90,32]{0,1:T(8,128)(2,1)S(1)} %get-tuple-element.8), channel_id=1, source_target_pairs={{0,4},{1,5},{2,6},{3,7},{4,0},{5,1},{6,2},{7,3},{8,12},{9,13},{10,... | collective-permute-start | bytes 17288 | tf_op jit(solution)/shard_map/ppermute | solution.py:24
  72.6 5.6 %collective-permute-start.4 = (bf16[90,32]{0,1:T(8,128)(2,1)S(1)}, bf16[90,32]{0,1:T(8,128)(2,1)S(1)}, u32[]{:S(2)}, u32[]{:S(2)}) collective-permute-start(bf16[90,32]{0,1:T(8,128)(2,1)S(1)} %get-tuple-element.7), channel_id=1, source_target_pairs={{0,5},{1,4},{2,7},{3,6},{4,1},{5,0},{6,3},{7,2},{8,13},{9,12},{10,... | collective-permute-start | bytes 17288 | tf_op jit(solution)/shard_map/ppermute | solution.py:24
  74.6 5.4 %collective-permute-start.5 = (bf16[90,32]{0,1:T(8,128)(2,1)S(1)}, bf16[90,32]{0,1:T(8,128)(2,1)S(1)}, u32[]{:S(2)}, u32[]{:S(2)}) collective-permute-start(bf16[90,32]{0,1:T(8,128)(2,1)S(1)} %get-tuple-element.6), channel_id=1, source_target_pairs={{0,6},{1,7},{2,4},{3,5},{4,2},{5,3},{6,0},{7,1},{8,14},{9,15},{10,... | collective-permute-start | bytes 17288 | tf_op jit(solution)/shard_map/ppermute | solution.py:24
  76.1 4.9 %collective-permute-start.6 = (bf16[90,32]{0,1:T(8,128)(2,1)S(1)}, bf16[90,32]{0,1:T(8,128)(2,1)S(1)}, u32[]{:S(2)}, u32[]{:S(2)}) collective-permute-start(bf16[90,32]{0,1:T(8,128)(2,1)S(1)} %get-tuple-element.5), channel_id=1, source_target_pairs={{0,7},{1,6},{2,5},{3,4},{4,3},{5,2},{6,1},{7,0},{8,15},{9,14},{10,... | collective-permute-start | bytes 17288 | tf_op jit(solution)/shard_map/ppermute | solution.py:24
Sparse Core Ops, SparseCore 0:
  9.2 33.0 all-gather.1
